TPU v7x, 32 devices: a whole 2x2x4 slice. The times are simulated.
32 devices in a mesh: gz: 4 (over y, x), gy: 2 (over core), gx: 4 (over z).
Axes of the slice: x: 2, y: 2, z: 4, core: 2. Of those that a mesh axis runs over, the one named last changes fastest.
Arguments:
- populations: float32 [19, 32, 16, 512], P(None, 'gz', 'gy', 'gx'), may hold values from 0.1 to 20, as said below
- solid: int32 [32, 16, 512], P('gz', 'gy', 'gx'), may hold values 0 or 1
- ports: int32 [2, 16, 512], P(None, 'gy', 'gx'), may hold values 0 or 1
- concentration: float32 [2, 4, 2, 64], P(None, 'gz'), may hold values from 0 to 1
- loaded: float32 [2, 4, 2, 64], P(None, 'gz'), may hold values from 0 to 2
Outputs:
- final_populations: float32 [19, 32, 16, 512], P(None, 'gz', 'gy', 'gx')
- new_concentration: float32 [2, 4, 2, 64], P(None, 'gz')
- new_loaded: float32 [2, 4, 2, 64], P(None, 'gz')
Inputs may be any that keep to these rules, and one draw needn't show every extreme that they name: `populations`: every population is positive and of the size of its lattice weight times 36.
All inputs are finite; a program needn't handle non-finite values. No bound on the sum of `solid` or of `ports` on one device may be relied on, other than what follows from the above.
Results may differ from a plain program's by a relative error of at most 0.00002.
Values sent between devices are 32-bit elements; how exact they have to be, the bound alone decides.
A program may use at most 64 MiB of HBM per device.

v0:
```python
import jax
import jax.numpy as jnp
from jax import lax
from jax.sharding import PartitionSpec as P

ITERS = 2
lattice = [
    (0, 0, 0),
    (1, 0, 0),
    (-1, 0, 0),
    (0, 1, 0),
    (0, -1, 0),
    (0, 0, 1),
    (0, 0, -1),
    (1, 1, 0),
    (-1, -1, 0),
    (1, -1, 0),
    (-1, 1, 0),
    (1, 0, 1),
    (-1, 0, -1),
    (1, 0, -1),
    (-1, 0, 1),
    (0, 1, 1),
    (0, -1, -1),
    (0, 1, -1),
    (0, -1, 1),
]
opposite = [0, 2, 1, 4, 3, 6, 5, 8, 7, 10, 9, 12, 11, 14, 13, 16, 15, 18, 17]
weights = [1.0 / 3.0] + [1.0 / 18.0] * 6 + [1.0 / 36.0] * 12
relax_rate = 1.25
base_density = 36.0
inlet_speed = 0.05
spread_base = (0.03, 0.06)
spread_length = 0.1
uptake_rate = (0.3, 0.6)
affinity = (2.0, 0.5)
phase_ratio = 0.5
feed_level = (1.0, 0.5)


def extended(cells, sides, width, closed):
    for axis, dim in sides:
        count = lax.axis_size(axis)
        ends = count if closed else count - 1
        head = lax.slice_in_dim(cells, 0, width, axis=dim)
        tail = lax.slice_in_dim(cells, cells.shape[dim] - width, cells.shape[dim], axis=dim)
        cells = jnp.concatenate(
            [
                lax.ppermute(tail, axis, [(i, (i + 1) % count) for i in range(ends)]),
                cells,
                lax.ppermute(head, axis, [((i + 1) % count, i) for i in range(ends)]),
            ],
            axis=dim,
        )
    return cells


def equilibrium(density, velocity):
    speed_z, speed_y, speed_x = velocity
    square = speed_z * speed_z + speed_y * speed_y + speed_x * speed_x
    result = []
    for member in range(19):
        step_z, step_y, step_x = lattice[member]
        along = step_z * speed_z + step_y * speed_y + step_x * speed_x
        result.append(
            weights[member] * density * (1.0 + 3.0 * along + 4.5 * along * along - 1.5 * square)
        )
    return result


def moments(pops):
    density = pops[0]
    for member in range(1, 19):
        density = density + pops[member]
    flows = []
    for position in range(3):
        total = jnp.zeros_like(pops[0])
        for member in range(19):
            heading = lattice[member][position]
            if heading == 1:
                total = total + pops[member]
            elif heading == -1:
                total = total - pops[member]
        flows.append(total)
    return (density, flows)


def collide(pops, solid_flag):
    density, flows = moments(pops)
    velocity = [flow / density for flow in flows]
    balance = equilibrium(density, velocity)
    post = [
        jnp.where(
            solid_flag,
            pops[opposite[member]],
            pops[member] - relax_rate * (pops[member] - balance[member]),
        )
        for member in range(19)
    ]
    return (post, velocity)


def close_ends(moved, post, velocity, ports, first_dev, last_dev):
    inflow = equilibrium(base_density, (inlet_speed, 0.0, 0.0))
    outflow = equilibrium(base_density, (velocity[0][-1], velocity[1][-1], velocity[2][-1]))
    inlet_open = ports[0] == 1
    outlet_open = ports[1] == 1
    result = list(moved)
    for member in range(19):
        step_z = lattice[member][0]
        back = post[opposite[member]]
        if step_z == 1:
            entering = jnp.where(inlet_open, inflow[member], back[0])
            result[member] = (
                result[member].at[0].set(jnp.where(first_dev, entering, result[member][0]))
            )
        elif step_z == -1:
            entering = jnp.where(outlet_open, outflow[member], back[-1])
            result[member] = (
                result[member].at[-1].set(jnp.where(last_dev, entering, result[member][-1]))
            )
    return result


def block_sum(field):
    depth, height, width = field.shape
    return field.reshape(depth // 8, 8, height // 8, 8, width // 8, 8).sum(axis=(1, 3, 5))


def transport(padded, loaded, coarse_vel):
    centre = padded[:, 1:-1]
    neighbours = [
        (padded[:, :-2], padded[:, 2:]),
        (jnp.roll(centre, 1, axis=2), jnp.roll(centre, -1, axis=2)),
        (jnp.roll(centre, 1, axis=3), jnp.roll(centre, -1, axis=3)),
    ]
    change = jnp.zeros_like(centre)
    curvature = jnp.zeros_like(centre)
    reach = jnp.zeros_like(coarse_vel[0])
    for direction in range(3):
        courant = 8.0 * coarse_vel[direction]
        before, after = neighbours[direction]
        change = (
            change
            - jnp.maximum(courant, 0.0) * (centre - before)
            - jnp.minimum(courant, 0.0) * (after - centre)
        )
        curvature = curvature + after - 2.0 * centre + before
        reach = reach + jnp.abs(courant)
    base = jnp.array(spread_base, dtype=centre.dtype)[:, None, None, None]
    speed = jnp.array(uptake_rate, dtype=centre.dtype)[:, None, None, None]
    holding = jnp.array(affinity, dtype=centre.dtype)[:, None, None, None]
    rate = speed * (holding * centre - loaded)
    new_conc = centre + change + (base + spread_length * reach) * curvature - phase_ratio * rate
    return (new_conc, loaded + rate)


def body(populations, solid, ports, concentration, loaded):
    depth, height, width = solid.shape
    slab_pos = lax.axis_index("gz")
    first_dev = slab_pos == 0
    last_dev = slab_pos == lax.axis_size("gz") - 1
    pops = [populations[member] for member in range(19)]
    solid_flag = solid == 1
    for iteration in range(ITERS):
        post, velocity = collide(pops, solid_flag)
        padded = extended(jnp.stack(post), (("gz", 1), ("gy", 2), ("gx", 3)), 1, True)
        moved = []
        for member in range(19):
            step_z, step_y, step_x = lattice[member]
            moved.append(
                padded[
                    member,
                    1 - step_z : 1 - step_z + depth,
                    1 - step_y : 1 - step_y + height,
                    1 - step_x : 1 - step_x + width,
                ]
            )
        pops = close_ends(moved, post, velocity, ports, first_dev, last_dev)
    final = jnp.stack(pops)
    density, flows = moments(pops)
    fluid = (solid == 0).astype(jnp.float32)
    local = jnp.stack([block_sum(flow * fluid) for flow in flows]) / (512.0 * base_density)
    across = lax.all_gather(local, "gy", axis=2, tiled=True)
    coarse_vel = lax.all_gather(across, "gx", axis=3, tiled=True)
    padded_conc = extended(concentration, (("gz", 1),), 1, False)
    feed = jnp.broadcast_to(
        jnp.array(feed_level, dtype=jnp.float32)[:, None, None],
        (2, concentration.shape[2], concentration.shape[3]),
    )
    front = jnp.where(first_dev, feed, padded_conc[:, 0])
    rear = jnp.where(last_dev, concentration[:, -1], padded_conc[:, -1])
    padded_conc = padded_conc.at[:, 0].set(front).at[:, -1].set(rear)
    new_conc, new_load = transport(padded_conc, loaded, coarse_vel)
    return (final, new_conc, new_load)


def solution(mesh):
    placed = (
        P(None, "gz", "gy", "gx"),
        P("gz", "gy", "gx"),
        P(None, "gy", "gx"),
        P(None, "gz", None, None),
        P(None, "gz", None, None),
    )
    return jax.shard_map(
        body,
        mesh=mesh,
        in_specs=placed,
        out_specs=(P(None, "gz", "gy", "gx"), P(None, "gz", None, None), P(None, "gz", None, None)),
        check_vma=False,
    )
```

profile of v0, /device:TPU:0, one launch (start us, length us, event | category | flops | bytes accessed | tf_op | source)
XLA Modules:
  0.0 104.6 jit_solution(4216951791328130897)
XLA Ops:
  0.6 5.6 %collective-permute-start.12 = (f32[2,1,2,64]{3,2,1,0:T(2,128)}, f32[2,1,2,64]{3,2,1,0:T(2,128)}, u32[]{:S(2)}, u32[]{:S(2)}) collective-permute-start(f32[2,1,2,64]{3,2,1,0:T(2,128)} %param.56), channel_id=1, source_target_pairs={{0,8},{8,16},{16,24},{1,9},{9,17},{17,25},{2,10},{10,18},{18,26},{... | collective-permute-start | bytes 3080 | tf_op jit(solution)/shard_map/ppermute | solution.py:49
  6.2 1.3 %collective-permute-start.13 = (f32[2,1,2,64]{3,2,1,0:T(2,128)}, f32[2,1,2,64]{3,2,1,0:T(2,128)}, u32[]{:S(2)}, u32[]{:S(2)}) collective-permute-start(f32[2,1,2,64]{3,2,1,0:T(2,128)} %param.56), channel_id=1, source_target_pairs={{8,0},{16,8},{24,16},{9,1},{17,9},{25,17},{10,2},{18,10},{26,18},{... | collective-permute-start | bytes 3080 | tf_op jit(solution)/shard_map/ppermute | solution.py:51
  7.5 1.2 %constant_dynamic-update-slice_fusion.18 = (f32[19,8,8,128]{3,2,1,0:T(8,128)S(1)}, f32[8,8,128]{2,1,0:T(8,128)S(1)}, f32[8,8,128]{2,1,0:T(8,128)S(1)}, f32[8,8,1...) fusion(f32[19,8,8,128]{3,2,1,0:T(8,128)} %param.53, ...), kind=kLoop, calls=%fused_computation.20 | loop fusion | flops 589823 | bytes 860160
  9.5 0.8 constant_dynamic-update-slice_fusion.16
  11.8 2.7 %collective-permute-start = (f32[19,1,8,128]{3,2,1,0:T(8,128)S(1)}, f32[19,1,8,128]{3,2,1,0:T(8,128)S(1)}, u32[]{:S(2)}, u32[]{:S(2)}) collective-permute-start(f32[19,1,8,128]{3,2,1,0:T(8,128)S(1)} %get-tuple-element.383), channel_id=1, source_target_pairs={{0,8},{8,16},{16,24},{24,0},{1,9},{9,17},{17,25},{25,1},{2,10},{10... | collective-permute-start | bytes 233480 | tf_op jit(solution)/shard_map/ppermute | solution.py:49
  14.5 1.0 collective-permute-start.1
  16.2 2.4 %collective-permute-done = f32[19,1,8,128]{3,2,1,0:T(8,128)S(1)} collective-permute-done((f32[19,1,8,128]{3,2,1,0:T(8,128)S(1)}, f32[19,1,8,128]{3,2,1,0:T(8,128)S(1)}, u32[]{:S(2)}, u32[]{:S(2)}) %collective-permute-start) | collective-permute-done | bytes 77856 | tf_op jit(solution)/shard_map/ppermute | solution.py:49
  18.6 0.9 collective-permute-done.1
  21.5 1.7 %fusion.386 = (f32[19,10,10,1]{3,2,1,0:T(8,128)}, f32[19,10,10,1]{3,2,1,0:T(8,128)S(1)}) fusion(f32[19,10,10,128]{3,2,1,0:T(8,128)S(1)} %pad_maximum_fusion), kind=kLoop, calls=%fused_computation.679 | loop fusion | bytes 30400 | tf_op jit(solution)/shard_map/slice | solution.py:45
  23.2 2.1 %copy.55 = f32[19,10,10,1]{0,3,2,1:T(1,128)S(1)} copy(f32[19,10,10,1]{3,2,1,0:T(8,128)} %get-tuple-element.355) | data formatting | bytes 15200 | tf_op jit(solution)/shard_map/slice | solution.py:45
  25.4 3.6 %collective-permute-start.5 = (f32[19,10,10,1]{0,3,2,1:T(1,128)S(1)}, f32[19,10,10,1]{0,3,2,1:T(1,128)S(1)}, u32[]{:S(2)}, u32[]{:S(2)}) collective-permute-start(f32[19,10,10,1]{0,3,2,1:T(1,128)S(1)} %copy.55), channel_id=1, source_target_pairs={{1,0},{2,1},{3,2},{0,3},{5,4},{6,5},{7,6},{4,7},{9,8},{10,9},{11,1... | collective-permute-start | bytes 22808 | tf_op jit(solution)/shard_map/ppermute | solution.py:51
  29.9 1.1 %collective-permute-done.5 = f32[19,10,10,1]{0,3,2,1:T(1,128)S(1)} collective-permute-done((f32[19,10,10,1]{0,3,2,1:T(1,128)S(1)}, f32[19,10,10,1]{0,3,2,1:T(1,128)S(1)}, u32[]{:S(2)}, u32[]{:S(2)}) %collective-permute-start.5) | collective-permute-done | bytes 7632 | tf_op jit(solution)/shard_map/ppermute | solution.py:51
  31.0 1.6 %copy.56 = f32[19,10,10,1]{3,2,1,0:T(8,128)S(1)} copy(f32[19,10,10,1]{0,3,2,1:T(1,128)S(1)} %collective-permute-done.5) | data formatting | bytes 15200 | tf_op jit(solution)/shard_map/ppermute | solution.py:51
  32.7 3.0 %collective-permute-done.4 = f32[19,10,10,1]{0,3,2,1:T(1,128)S(1)} collective-permute-done((f32[19,10,10,1]{0,3,2,1:T(1,128)S(1)}, f32[19,10,10,1]{0,3,2,1:T(1,128)S(1)}, u32[]{:S(2)}, u32[]{:S(2)}) %collective-permute-start.4) | collective-permute-done | bytes 7632 | tf_op jit(solution)/shard_map/ppermute | solution.py:49
  35.7 2.7 %copy.54 = f32[19,10,10,1]{3,2,1,0:T(8,128)} copy(f32[19,10,10,1]{0,3,2,1:T(1,128)S(1)} %collective-permute-done.4) | data formatting | bytes 15200 | tf_op jit(solution)/shard_map/ppermute | solution.py:49
  38.4 1.0 maximum_bitcast_fusion.13
  39.5 1.3 %copy-done = f32[19,10,10,1]{3,2,1,0:T(8,128)S(1)} copy-done((f32[19,10,10,1]{3,2,1,0:T(8,128)S(1)}, f32[19,10,10,1]{3,2,1,0:T(8,128)}, u32[]{:S(2)}) %copy-start) | copy-done | bytes 7624
  48.5 2.1 %collective-permute-start.6 = (f32[19,1,8,128]{3,2,1,0:T(8,128)S(1)}, f32[19,1,8,128]{3,2,1,0:T(8,128)S(1)}, u32[]{:S(2)}, u32[]{:S(2)}) collective-permute-start(f32[19,1,8,128]{3,2,1,0:T(8,128)S(1)} %get-tuple-element.382), channel_id=1, source_target_pairs={{0,8},{8,16},{16,24},{24,0},{1,9},{9,17},{17,25},{25,1},{2,10},{10... | collective-permute-start | bytes 233480 | tf_op jit(solution)/shard_map/ppermute | solution.py:49
  50.6 0.8 collective-permute-start.7
  52.1 1.7 %collective-permute-done.6 = f32[19,1,8,128]{3,2,1,0:T(8,128)S(1)} collective-permute-done((f32[19,1,8,128]{3,2,1,0:T(8,128)S(1)}, f32[19,1,8,128]{3,2,1,0:T(8,128)S(1)}, u32[]{:S(2)}, u32[]{:S(2)}) %collective-permute-start.6) | collective-permute-done | bytes 77856 | tf_op jit(solution)/shard_map/ppermute | solution.py:49
  53.8 1.2 %collective-permute-done.7 = f32[19,1,8,128]{3,2,1,0:T(8,128)S(1)} collective-permute-done((f32[19,1,8,128]{3,2,1,0:T(8,128)S(1)}, f32[19,1,8,128]{3,2,1,0:T(8,128)S(1)}, u32[]{:S(2)}, u32[]{:S(2)}) %collective-permute-start.7) | collective-permute-done | bytes 77856 | tf_op jit(solution)/shard_map/ppermute | solution.py:51
  57.0 1.7 %fusion.385 = (f32[19,10,10,1]{3,2,1,0:T(8,128)S(1)}, f32[19,10,10,1]{3,2,1,0:T(8,128)}) fusion(f32[19,10,10,128]{3,2,1,0:T(8,128)S(1)} %pad_maximum_fusion.1), kind=kLoop, calls=%fused_computation.678 | loop fusion | bytes 30400 | tf_op jit(solution)/shard_map/slice | solution.py:45
  58.7 2.1 %copy.57 = f32[19,10,10,1]{0,3,2,1:T(1,128)S(1)} copy(f32[19,10,10,1]{3,2,1,0:T(8,128)} %get-tuple-element.354) | data formatting | bytes 15200 | tf_op jit(solution)/shard_map/slice | solution.py:46
  61.6 4.0 %collective-permute-start.11 = (f32[19,10,10,1]{0,3,2,1:T(1,128)S(1)}, f32[19,10,10,1]{0,3,2,1:T(1,128)}, u32[]{:S(2)}, u32[]{:S(2)}) collective-permute-start(f32[19,10,10,1]{0,3,2,1:T(1,128)S(1)} %copy.59), channel_id=1, source_target_pairs={{1,0},{2,1},{3,2},{0,3},{5,4},{6,5},{7,6},{4,7},{9,8},{10,9},{11,1... | collective-permute-start | bytes 22808 | tf_op jit(solution)/shard_map/ppermute | solution.py:51
  65.7 1.7 %collective-permute-done.11 = f32[19,10,10,1]{0,3,2,1:T(1,128)} collective-permute-done((f32[19,10,10,1]{0,3,2,1:T(1,128)S(1)}, f32[19,10,10,1]{0,3,2,1:T(1,128)}, u32[]{:S(2)}, u32[]{:S(2)}) %collective-permute-start.11) | collective-permute-done | bytes 7632 | tf_op jit(solution)/shard_map/ppermute | solution.py:51
  67.4 2.4 %copy.60 = f32[19,10,10,1]{3,2,1,0:T(8,128)S(1)} copy(f32[19,10,10,1]{0,3,2,1:T(1,128)} %collective-permute-done.11) | data formatting | bytes 15200 | tf_op jit(solution)/shard_map/ppermute | solution.py:51
  71.8 3.4 %copy.58 = f32[19,10,10,1]{3,2,1,0:T(8,128)} copy(f32[19,10,10,1]{0,3,2,1:T(1,128)} %collective-permute-done.10) | data formatting | bytes 15200 | tf_op jit(solution)/shard_map/ppermute | solution.py:49
  75.3 1.1 %maximum_bitcast_fusion.3 = (f32[8,8,128]{2,1,0:T(8,128)S(1)}, f32[8,8,128]{2,1,0:T(8,128)S(1)}, f32[8,8,128]{2,1,0:T(8,128)S(1)}) fusion(f32[19,10,10,1]{3,2,1,0:T(8,128)} %copy.58, f32[19,10,1,128]{3,2,1,0:T(1,128)S(1)} %collective-permute-done.9, f32[19,10,1,128]{3,2,1,0:T(1,128)S(1)} %collective-permute-done.8, ...), kind=kLoop, calls=%fused_computation.399 | loop fusion | flops 106496 | bytes 1078704 | tf_op jit(solution)/shard_map/squeeze | solution.py:172
  80.5 1.4 %select_reduce_fusion = (f32[128]{0:T(128)}, f32[128]{0:T(128)S(1)}, f32[128]{0:T(128)}, f32[1,8,8,128]{3,2,1,0:T(8,128)S(1)}, f32[1,8,8,128]{3,2,1,0:T(8,128)S(...) fusion(f32[8,8,128]{2,1,0:T(8,128)S(1)} %get-tuple-element.278,, ...), kind=kLoop, calls=%fused_computation.509 | loop fusion | flops 573056 | bytes 1612128 | tf_op jit(solution)/shard_map/reduce_sum | solution.py:127
  83.9 1.8 %all_gather.6 = f32[3,1,2,16]{3,1,0,2:T(1,128)S(1)} all-gather(f32[3,1,1,16]{3,1,0,2:T(1,128)S(1)} %fusion.358), channel_id=1, replica_groups=mesh['gz'=4,'gy'=2,'gx'=4] {'gy'}, dimensions={2}, use_global_device_ids=true | all-gather | bytes 576 | tf_op jit(solution)/shard_map/all_gather | solution.py:184
  85.8 13.6 %all_gather.7 = f32[3,1,2,64]{0,2,1,3:T(2,128)S(1)} all-gather(f32[3,1,2,16]{0,2,1,3:T(2,128)S(1)} %copy.62), channel_id=1, replica_groups=mesh['gz'=4,'gy'=2,'gx'=4] {'gx'}, dimensions={3}, use_global_device_ids=true | all-gather | bytes 1920 | tf_op jit(solution)/shard_map/all_gather | solution.py:185
  103.3 1.4 %multiply_subtract_fusion = f32[2,1,2,64]{3,2,1,0:T(2,128)} fusion(f32[2,1,2,64]{3,2,1,0:T(2,128)S(1)} %copy-done.9, f32[2,1,2,1]{3,2,1,0:T(2,128)S(1)} %copy-done.19, f32[2,1,2,63]{3,2,1,0:T(2,128)S(1)} %copy-done.21, f32[2,1,2,63]{3,2,1,0:T(2,128)S(1)} %copy-done.20, f32[2,1,2,1]{3,2,1,0:T(2,128)S(1)} %copy-done.18, f32[2,1,1,64]{3,2,1,0:T(1,128)S(1)} %copy-done.23, ...), kind=kLoop, calls=%fused_computation.666 | loop fusion | flops 10496 | bytes 11810 | tf_op jit(solution)/shard_map/sub | solution.py:154
  (170 shorter events, 28.7 us)
Async XLA Ops:
  0.6 10.5 %copy-start.2 = (f32[19,8,8,128]{3,2,1,0:T(8,128)S(1)}, f32[19,8,8,128]{3,2,1,0:T(8,128)}, u32[]{:S(2)}) copy-start(f32[19,8,8,128]{3,2,1,0:T(8,128)} %param.53) | copy-start | bytes 1867780
  0.6 102.5 %collective-permute-start.12 = (f32[2,1,2,64]{3,2,1,0:T(2,128)}, f32[2,1,2,64]{3,2,1,0:T(2,128)}, u32[]{:S(2)}, u32[]{:S(2)}) collective-permute-start(f32[2,1,2,64]{3,2,1,0:T(2,128)} %param.56), channel_id=1, source_target_pairs={{0,8},{8,16},{16,24},{1,9},{9,17},{17,25},{2,10},{10,18},{18,26},{... | collective-permute-start | bytes 3080 | tf_op jit(solution)/shard_map/ppermute | solution.py:49
  6.2 96.9 %collective-permute-start.13 = (f32[2,1,2,64]{3,2,1,0:T(2,128)}, f32[2,1,2,64]{3,2,1,0:T(2,128)}, u32[]{:S(2)}, u32[]{:S(2)}) collective-permute-start(f32[2,1,2,64]{3,2,1,0:T(2,128)} %param.56), channel_id=1, source_target_pairs={{8,0},{16,8},{24,16},{9,1},{17,9},{25,17},{10,2},{18,10},{26,18},{... | collective-permute-start | bytes 3080 | tf_op jit(solution)/shard_map/ppermute | solution.py:51
  11.3 4.3 %copy-start.8 = (f32[2,1,2,64]{3,2,1,0:T(2,128)S(1)}, f32[2,1,2,64]{3,2,1,0:T(2,128)}, u32[]{:S(2)}) copy-start(f32[2,1,2,64]{3,2,1,0:T(2,128)} %param.56) | copy-start | bytes 3076
  11.3 4.2 %copy-start.16 = (f32[2,1,2,64]{3,2,1,0:T(2,128)S(1)}, f32[2,1,2,64]{3,2,1,0:T(2,128)}, u32[]{:S(2)}) copy-start(f32[2,1,2,64]{3,2,1,0:T(2,128)} %param.57) | copy-start | bytes 3076
  11.8 6.8 %collective-permute-start = (f32[19,1,8,128]{3,2,1,0:T(8,128)S(1)}, f32[19,1,8,128]{3,2,1,0:T(8,128)S(1)}, u32[]{:S(2)}, u32[]{:S(2)}) collective-permute-start(f32[19,1,8,128]{3,2,1,0:T(8,128)S(1)} %get-tuple-element.383), channel_id=1, source_target_pairs={{0,8},{8,16},{16,24},{24,0},{1,9},{9,17},{17,25},{25,1},{2,10},{10... | collective-permute-start | bytes 233480 | tf_op jit(solution)/shard_map/ppermute | solution.py:49
  14.5 5.0 %collective-permute-start.1 = (f32[19,1,8,128]{3,2,1,0:T(8,128)S(1)}, f32[19,1,8,128]{3,2,1,0:T(8,128)S(1)}, u32[]{:S(2)}, u32[]{:S(2)}) collective-permute-start(f32[19,1,8,128]{3,2,1,0:T(8,128)S(1)} %get-tuple-element.384), channel_id=1, source_target_pairs={{8,0},{16,8},{24,16},{0,24},{9,1},{17,9},{25,17},{1,25},{10,2},{18... | collective-permute-start | bytes 233480 | tf_op jit(solution)/shard_map/ppermute | solution.py:51
  19.7 1.4 %collective-permute-start.2 = (f32[19,10,1,128]{3,2,1,0:T(1,128)S(1)}, f32[19,10,1,128]{3,2,1,0:T(1,128)S(1)}, u32[]{:S(2)}, u32[]{:S(2)}) collective-permute-start(f32[19,10,1,128]{3,2,1,0:T(1,128)S(1)} %get-tuple-element.375), channel_id=1, source_target_pairs={{0,4},{4,0},{1,5},{5,1},{2,6},{6,2},{3,7},{7,3},{8,12},{12,8},{9,1... | collective-permute-start | bytes 291848 | tf_op jit(solution)/shard_map/ppermute | solution.py:49
  19.8 1.4 %collective-permute-start.3 = (f32[19,10,1,128]{3,2,1,0:T(1,128)S(1)}, f32[19,10,1,128]{3,2,1,0:T(1,128)S(1)}, u32[]{:S(2)}, u32[]{:S(2)}) collective-permute-start(f32[19,10,1,128]{3,2,1,0:T(1,128)S(1)} %get-tuple-element.376), channel_id=1, source_target_pairs={{4,0},{0,4},{5,1},{1,5},{6,2},{2,6},{7,3},{3,7},{12,8},{8,12},{13,... | collective-permute-start | bytes 291848 | tf_op jit(solution)/shard_map/ppermute | solution.py:51
  25.4 4.5 %copy-start.15 = (s32[2,8,128]{2,1,0:T(8,128)S(1)}, s32[2,8,128]{2,1,0:T(8,128)}, u32[]{:S(2)}) copy-start(s32[2,8,128]{2,1,0:T(8,128)} %param.55) | copy-start | bytes 24580
  25.4 5.6 %collective-permute-start.5 = (f32[19,10,10,1]{0,3,2,1:T(1,128)S(1)}, f32[19,10,10,1]{0,3,2,1:T(1,128)S(1)}, u32[]{:S(2)}, u32[]{:S(2)}) collective-permute-start(f32[19,10,10,1]{0,3,2,1:T(1,128)S(1)} %copy.55), channel_id=1, source_target_pairs={{1,0},{2,1},{3,2},{0,3},{5,4},{6,5},{7,6},{4,7},{9,8},{10,9},{11,1... | collective-permute-start | bytes 22808 | tf_op jit(solution)/shard_map/ppermute | solution.py:51
  29.8 5.9 %collective-permute-start.4 = (f32[19,10,10,1]{0,3,2,1:T(1,128)S(1)}, f32[19,10,10,1]{0,3,2,1:T(1,128)S(1)}, u32[]{:S(2)}, u32[]{:S(2)}) collective-permute-start(f32[19,10,10,1]{0,3,2,1:T(1,128)S(1)} %copy.53), channel_id=1, source_target_pairs={{0,1},{1,2},{2,3},{3,0},{4,5},{5,6},{6,7},{7,4},{8,9},{9,10},{10,1... | collective-permute-start | bytes 22808 | tf_op jit(solution)/shard_map/ppermute | solution.py:49
  29.9 11.0 %copy-start.10 = (pred[1,8,128]{2,1,0:T(8,128)(4,1)}, pred[1,8,128]{2,1,0:T(8,128)(4,1)S(1)}, u32[]{:S(2)}) copy-start(pred[1,8,128]{2,1,0:T(8,128)(4,1)S(1)} %get-tuple-element.317) | copy-start | bytes 3076
  48.5 5.3 %collective-permute-start.6 = (f32[19,1,8,128]{3,2,1,0:T(8,128)S(1)}, f32[19,1,8,128]{3,2,1,0:T(8,128)S(1)}, u32[]{:S(2)}, u32[]{:S(2)}) collective-permute-start(f32[19,1,8,128]{3,2,1,0:T(8,128)S(1)} %get-tuple-element.382), channel_id=1, source_target_pairs={{0,8},{8,16},{16,24},{24,0},{1,9},{9,17},{17,25},{25,1},{2,10},{10... | collective-permute-start | bytes 233480 | tf_op jit(solution)/shard_map/ppermute | solution.py:49
  50.6 4.4 %collective-permute-start.7 = (f32[19,1,8,128]{3,2,1,0:T(8,128)S(1)}, f32[19,1,8,128]{3,2,1,0:T(8,128)S(1)}, u32[]{:S(2)}, u32[]{:S(2)}) collective-permute-start(f32[19,1,8,128]{3,2,1,0:T(8,128)S(1)} %get-tuple-element.381), channel_id=1, source_target_pairs={{8,0},{16,8},{24,16},{0,24},{9,1},{17,9},{25,17},{1,25},{10,2},{18... | collective-permute-start | bytes 233480 | tf_op jit(solution)/shard_map/ppermute | solution.py:51
  55.2 1.4 %collective-permute-start.8 = (f32[19,10,1,128]{3,2,1,0:T(1,128)S(1)}, f32[19,10,1,128]{3,2,1,0:T(1,128)S(1)}, u32[]{:S(2)}, u32[]{:S(2)}) collective-permute-start(f32[19,10,1,128]{3,2,1,0:T(1,128)S(1)} %get-tuple-element.371), channel_id=1, source_target_pairs={{0,4},{4,0},{1,5},{5,1},{2,6},{6,2},{3,7},{7,3},{8,12},{12,8},{9,1... | collective-permute-start | bytes 291848 | tf_op jit(solution)/shard_map/ppermute | solution.py:49
  55.2 1.4 %collective-permute-start.9 = (f32[19,10,1,128]{3,2,1,0:T(1,128)S(1)}, f32[19,10,1,128]{3,2,1,0:T(1,128)S(1)}, u32[]{:S(2)}, u32[]{:S(2)}) collective-permute-start(f32[19,10,1,128]{3,2,1,0:T(1,128)S(1)} %get-tuple-element.372), channel_id=1, source_target_pairs={{4,0},{0,4},{5,1},{1,5},{6,2},{2,6},{7,3},{3,7},{12,8},{8,12},{13,... | collective-permute-start | bytes 291848 | tf_op jit(solution)/shard_map/ppermute | solution.py:51
  60.8 10.4 %collective-permute-start.10 = (f32[19,10,10,1]{0,3,2,1:T(1,128)S(1)}, f32[19,10,10,1]{0,3,2,1:T(1,128)}, u32[]{:S(2)}, u32[]{:S(2)}) collective-permute-start(f32[19,10,10,1]{0,3,2,1:T(1,128)S(1)} %copy.57), channel_id=1, source_target_pairs={{0,1},{1,2},{2,3},{3,0},{4,5},{5,6},{6,7},{7,4},{8,9},{9,10},{10,1... | collective-permute-start | bytes 22808 | tf_op jit(solution)/shard_map/ppermute | solution.py:49
  61.6 5.8 %collective-permute-start.11 = (f32[19,10,10,1]{0,3,2,1:T(1,128)S(1)}, f32[19,10,10,1]{0,3,2,1:T(1,128)}, u32[]{:S(2)}, u32[]{:S(2)}) collective-permute-start(f32[19,10,10,1]{0,3,2,1:T(1,128)S(1)} %copy.59), channel_id=1, source_target_pairs={{1,0},{2,1},{3,2},{0,3},{5,4},{6,5},{7,6},{4,7},{9,8},{10,9},{11,1... | collective-permute-start | bytes 22808 | tf_op jit(solution)/shard_map/ppermute | solution.py:51
  81.8 21.2 %copy-start.6 = (f32[1,8,8,128]{3,2,1,0:T(8,128)S(1)}, f32[1,8,8,128]{3,2,1,0:T(8,128)}, u32[]{:S(2)}) copy-start(f32[1,8,8,128]{3,2,1,0:T(8,128)} %get-tuple-element.273) | copy-start | bytes 98308
  81.8 21.3 %copy-start.9 = (f32[2,1,2,64]{3,2,1,0:T(2,128)S(1)}, f32[2,1,2,64]{3,2,1,0:T(2,128)}, u32[]{:S(2)}) copy-start(f32[2,1,2,64]{3,2,1,0:T(2,128)} %param.56) | copy-start | bytes 3076
  81.8 21.3 %copy-start.17 = (f32[2,1,2,64]{3,2,1,0:T(2,128)S(1)}, f32[2,1,2,64]{3,2,1,0:T(2,128)}, u32[]{:S(2)}) copy-start(f32[2,1,2,64]{3,2,1,0:T(2,128)} %param.57) | copy-start | bytes 3076
  81.8 21.3 %copy-start.18 = (f32[2,1,2,1]{3,2,1,0:T(2,128)S(1)}, f32[2,1,2,1]{3,2,1,0:T(2,128)}, u32[]{:S(2)}) copy-start(f32[2,1,2,1]{3,2,1,0:T(2,128)} %get-tuple-element.394) | copy-start | bytes 52
  81.8 21.3 %copy-start.19 = (f32[2,1,2,1]{3,2,1,0:T(2,128)S(1)}, f32[2,1,2,1]{3,2,1,0:T(2,128)}, u32[]{:S(2)}) copy-start(f32[2,1,2,1]{3,2,1,0:T(2,128)} %get-tuple-element.395) | copy-start | bytes 52
  81.9 21.3 %copy-start.20 = (f32[2,1,2,63]{3,2,1,0:T(2,128)S(1)}, f32[2,1,2,63]{3,2,1,0:T(2,128)}, u32[]{:S(2)}) copy-start(f32[2,1,2,63]{3,2,1,0:T(2,128)} %get-tuple-element.396) | copy-start | bytes 3028
  81.9 21.3 %copy-start.21 = (f32[2,1,2,63]{3,2,1,0:T(2,128)S(1)}, f32[2,1,2,63]{3,2,1,0:T(2,128)}, u32[]{:S(2)}) copy-start(f32[2,1,2,63]{3,2,1,0:T(2,128)} %get-tuple-element.397) | copy-start | bytes 3028
  81.9 21.3 %copy-start.22 = (f32[2,1,1,64]{3,2,1,0:T(1,128)S(1)}, f32[2,1,1,64]{3,2,1,0:T(1,128)}, u32[]{:S(2)}) copy-start(f32[2,1,1,64]{3,2,1,0:T(1,128)} %get-tuple-element.392) | copy-start | bytes 1540
  81.9 21.3 %copy-start.23 = (f32[2,1,1,64]{3,2,1,0:T(1,128)S(1)}, f32[2,1,1,64]{3,2,1,0:T(1,128)}, u32[]{:S(2)}) copy-start(f32[2,1,1,64]{3,2,1,0:T(1,128)} %get-tuple-element.393) | copy-start | bytes 1540
  81.9 21.3 %copy-start.25 = (f32[2]{0:T(128)S(1)}, f32[2]{0:T(128)}, u32[]{:S(2)}) copy-start(f32[2]{0:T(128)} %constant.557.clone) | copy-start | bytes 28
  81.9 21.3 %copy-start.27 = (f32[2]{0:T(128)S(1)}, f32[2]{0:T(128)}, u32[]{:S(2)}) copy-start(f32[2]{0:T(128)} %constant.558.clone) | copy-start | bytes 28
  81.9 21.3 %copy-start.28 = (f32[2]{0:T(128)S(1)}, f32[2]{0:T(128)}, u32[]{:S(2)}) copy-start(f32[2]{0:T(128)} %constant.555.clone) | copy-start | bytes 28
  81.9 21.3 %copy-start.29 = (f32[2]{0:T(128)S(1)}, f32[2]{0:T(128)}, u32[]{:S(2)}) copy-start(f32[2]{0:T(128)} %constant.556.clone) | copy-start | bytes 28
  (12 other events, 20.7 us)
where the time goes:
time: 106 us; the launch traced here: 105 us
  local copies, waits for them, and re-layouts  29.9 us (28%)
  other arithmetic  22.8 us (22%)
  starting transfers between devices  22.4 us (21%)
  blocking collectives  15.5 us (15%)
  waiting for transfers between devices  12.7 us (12%)
  between operations  1.35 us (1%)
    all_gather x1, blocking collectives, body(): coarse_vel = lax.all_gather(across, 'gx', axis=3, tiled=True)  13.6 us
    ppermute x7, starting transfers between devices, extended(): lax.ppermute(head, axis, [((i + 1) % count, i) for i in range(ends)])  11.8 us
    unnamed x35, other arithmetic  10.8 us
    ppermute x7, starting transfers between devices, extended(): lax.ppermute(tail, axis, [(i, (i + 1) % count) for i in range(ends)])  10.6 us
    ppermute x7, waiting for transfers between devices, extended(): lax.ppermute(tail, axis, [(i, (i + 1) % count) for i in range(ends)])  7.47 us
    unnamed x82, local copies, waits for them, and re-layouts  6.83 us
    slice x5, local copies, waits for them, and re-layouts, extended(): head = lax.slice_in_dim(cells, 0, width, axis=dim)  6.35 us
    ppermute x2, local copies, waits for them, and re-layouts, extended(): lax.ppermute(tail, axis, [(i, (i + 1) % count) for i in range(ends)])  6.09 us
  transfers between devices with their start and end apart: 14, of which 11 were waited for; matrix products, arithmetic and copies ran while one was open for 46% of the time, Pallas kernels for 0%

commit v1 on v0

--- a/solution.py
+++ b/solution.py
@@ -38,6 +38,12 @@
 feed_level = (1.0, 0.5)
 
 
+def laid_out(tiles, dim):
+    shape = list(tiles.shape[1:])
+    shape[dim] *= tiles.shape[0]
+    return jnp.moveaxis(tiles, 0, dim).reshape(shape)
+
+
 def extended(cells, sides, width, closed):
     for axis, dim in sides:
         count = lax.axis_size(axis)
@@ -182,7 +188,19 @@
     fluid = (solid == 0).astype(jnp.float32)
     local = jnp.stack([block_sum(flow * fluid) for flow in flows]) / (512.0 * base_density)
     across = lax.all_gather(local, "gy", axis=2, tiled=True)
-    coarse_vel = lax.all_gather(across, "gx", axis=3, tiled=True)
+    length = lax.axis_size("gx")
+    pairs = [(i_2, (i_2 + 1) % length) for i_2 in range(length)]
+    back_2 = [(b, a) for a, b in pairs]
+    lower, upper = ([], [])
+    for step in range(length - 1):
+        if step % 2 == 0:
+            lower.append(lax.ppermute(lower[-1] if lower else across, "gx", pairs))
+        else:
+            upper.append(lax.ppermute(upper[-1] if upper else across, "gx", back_2))
+    blocks = jnp.stack([*lower[::-1], across, *upper])
+    shift = lax.axis_index("gx") - len(lower)
+    blocks = blocks[(jnp.arange(length) - shift) % length]
+    coarse_vel = laid_out(blocks, 3)
     padded_conc = extended(concentration, (("gz", 1),), 1, False)
     feed = jnp.broadcast_to(
         jnp.array(feed_level, dtype=jnp.float32)[:, None, None],

time: 106 us -> 102 us (0.962)
  blocking collectives: 15.5 us -> 1.83 us
  starting transfers between devices: 22.4 us -> 26.2 us
  waiting for transfers between devices: 12.7 us -> 15.8 us
  other arithmetic: 22.8 us -> 24.2 us
  local copies, waits for them, and re-layouts: 29.9 us -> 31.1 us
    all_gather x1 -> x0, blocking collectives: 13.6 us -> none  [body(): coarse_vel = lax.all_gather(across, 'gx', axis=3, tiled=True)]
    ppermute x0 -> x3, waiting for transfers between devices: none -> 5.32 us  [the longest x2 5.31 us: body(): lower.append(lax.ppermute(lower[-1] if lower else across, 'gx', pairs))]
    ppermute x0 -> x3, starting transfers between devices: none -> 3.92 us  [the longest x1 3.83 us: body(): upper.append(lax.ppermute(upper[-1] if upper else across, 'gx', back_2))]
    ppermute x2, local copies, waits for them, and re-layouts: 6.09 us -> 4.26 us  [extended(): lax.ppermute(tail, axis, [(i, (i + 1) % count) for i in range(ends)])]
    ppermute x7, waiting for transfers between devices: 5.23 us -> 3.44 us  [extended(): lax.ppermute(head, axis, [((i + 1) % count, i) for i in range(ends)])]
    unnamed x82 -> x53, local copies, waits for them, and re-layouts: 6.83 us -> 6.51 us
  transfers between devices with their start and end apart: 14 -> 17, of which waited for: 11 -> 12; matrix products, arithmetic and copies ran while one was open for 46% -> 52% of each run, Pallas kernels for 0% -> 0%
where the time goes in v1:
time: 102 us; the launch traced here: 100 us
  local copies, waits for them, and re-layouts  31.1 us (30%)
  starting transfers between devices  26.2 us (26%)
  other arithmetic  24.2 us (24%)
  waiting for transfers between devices  15.8 us (15%)
  blocking collectives  1.83 us (2%)
  between operations  1.2 us (1%)
    ppermute x7, starting transfers between devices, extended(): lax.ppermute(head, axis, [((i + 1) % count, i) for i in range(ends)])  11.6 us
    unnamed x35, other arithmetic  10.8 us
    ppermute x7, starting transfers between devices, extended(): lax.ppermute(tail, axis, [(i, (i + 1) % count) for i in range(ends)])  10.6 us
    ppermute x7, waiting for transfers between devices, extended(): lax.ppermute(tail, axis, [(i, (i + 1) % count) for i in range(ends)])  7.02 us
    slice x5, local copies, waits for them, and re-layouts, extended(): head = lax.slice_in_dim(cells, 0, width, axis=dim)  6.98 us
    unnamed x53, local copies, waits for them, and re-layouts  6.51 us
    ppermute x2, waiting for transfers between devices, body(): lower.append(lax.ppermute(lower[-1] if lower else across, 'gx', pairs))  5.31 us
    ppermute x2, local copies, waits for them, and re-layouts, extended(): lax.ppermute(head, axis, [((i + 1) % count, i) for i in range(ends)])  5.04 us
  transfers between devices with their start and end apart: 17, of which 12 were waited for; matrix products, arithmetic and copies ran while one was open for 52% of the time, Pallas kernels for 0%

profile of v1, /device:TPU:0, one launch (start us, length us, event | category | flops | bytes accessed | tf_op | source)
XLA Modules:
  0.0 100.3 jit_solution(13747544099414269072)
XLA Ops:
  0.6 5.6 %collective-permute-start.15 = (f32[2,1,2,64]{3,2,1,0:T(2,128)}, f32[2,1,2,64]{3,2,1,0:T(2,128)}, u32[]{:S(2)}, u32[]{:S(2)}) collective-permute-start(f32[2,1,2,64]{3,2,1,0:T(2,128)} %param.56), channel_id=1, source_target_pairs={{0,8},{8,16},{16,24},{1,9},{9,17},{17,25},{2,10},{10,18},{18,26},{... | collective-permute-start | bytes 3080 | tf_op jit(solution)/shard_map/ppermute | solution.py:55
  6.2 1.3 %collective-permute-start.16 = (f32[2,1,2,64]{3,2,1,0:T(2,128)}, f32[2,1,2,64]{3,2,1,0:T(2,128)}, u32[]{:S(2)}, u32[]{:S(2)}) collective-permute-start(f32[2,1,2,64]{3,2,1,0:T(2,128)} %param.56), channel_id=1, source_target_pairs={{8,0},{16,8},{24,16},{9,1},{17,9},{25,17},{10,2},{18,10},{26,18},{... | collective-permute-start | bytes 3080 | tf_op jit(solution)/shard_map/ppermute | solution.py:57
  7.5 1.2 %constant_dynamic-update-slice_fusion.18 = (f32[19,8,8,128]{3,2,1,0:T(8,128)S(1)}, f32[8,8,128]{2,1,0:T(8,128)S(1)}, f32[8,8,128]{2,1,0:T(8,128)S(1)}, f32[8,8,1...) fusion(f32[19,8,8,128]{3,2,1,0:T(8,128)} %param.53, ...), kind=kLoop, calls=%fused_computation.21 | loop fusion | flops 589823 | bytes 860160
  11.8 2.7 %collective-permute-start = (f32[19,1,8,128]{3,2,1,0:T(8,128)S(1)}, f32[19,1,8,128]{3,2,1,0:T(8,128)S(1)}, u32[]{:S(2)}, u32[]{:S(2)}) collective-permute-start(f32[19,1,8,128]{3,2,1,0:T(8,128)S(1)} %get-tuple-element.383), channel_id=1, source_target_pairs={{0,8},{8,16},{16,24},{24,0},{1,9},{9,17},{17,25},{25,1},{2,10},{10... | collective-permute-start | bytes 233480 | tf_op jit(solution)/shard_map/ppermute | solution.py:55
  14.5 1.0 %collective-permute-start.1 = (f32[19,1,8,128]{3,2,1,0:T(8,128)S(1)}, f32[19,1,8,128]{3,2,1,0:T(8,128)S(1)}, u32[]{:S(2)}, u32[]{:S(2)}) collective-permute-start(f32[19,1,8,128]{3,2,1,0:T(8,128)S(1)} %get-tuple-element.384), channel_id=1, source_target_pairs={{8,0},{16,8},{24,16},{0,24},{9,1},{17,9},{25,17},{1,25},{10,2},{18... | collective-permute-start | bytes 233480 | tf_op jit(solution)/shard_map/ppermute | solution.py:57
  17.5 1.1 %collective-permute-done = f32[19,1,8,128]{3,2,1,0:T(8,128)S(1)} collective-permute-done((f32[19,1,8,128]{3,2,1,0:T(8,128)S(1)}, f32[19,1,8,128]{3,2,1,0:T(8,128)S(1)}, u32[]{:S(2)}, u32[]{:S(2)}) %collective-permute-start) | collective-permute-done | bytes 77856 | tf_op jit(solution)/shard_map/ppermute | solution.py:55
  18.6 0.9 collective-permute-done.1
  21.5 1.7 %fusion.394 = (f32[19,10,10,1]{3,2,1,0:T(8,128)}, f32[19,10,10,1]{3,2,1,0:T(8,128)S(1)}) fusion(f32[19,10,10,128]{3,2,1,0:T(8,128)S(1)} %pad_maximum_fusion), kind=kLoop, calls=%fused_computation.696 | loop fusion | bytes 30400 | tf_op jit(solution)/shard_map/slice | solution.py:51
  23.2 2.1 %copy.88 = f32[19,10,10,1]{0,3,2,1:T(1,128)S(1)} copy(f32[19,10,10,1]{3,2,1,0:T(8,128)} %get-tuple-element.355) | data formatting | bytes 15200 | tf_op jit(solution)/shard_map/slice | solution.py:51
  25.4 3.6 %collective-permute-start.5 = (f32[19,10,10,1]{0,3,2,1:T(1,128)S(1)}, f32[19,10,10,1]{0,3,2,1:T(1,128)S(1)}, u32[]{:S(2)}, u32[]{:S(2)}) collective-permute-start(f32[19,10,10,1]{0,3,2,1:T(1,128)S(1)} %copy.88), channel_id=1, source_target_pairs={{1,0},{2,1},{3,2},{0,3},{5,4},{6,5},{7,6},{4,7},{9,8},{10,9},{11,1... | collective-permute-start | bytes 22808 | tf_op jit(solution)/shard_map/ppermute | solution.py:57
  29.9 1.0 %collective-permute-done.5 = f32[19,10,10,1]{0,3,2,1:T(1,128)S(1)} collective-permute-done((f32[19,10,10,1]{0,3,2,1:T(1,128)S(1)}, f32[19,10,10,1]{0,3,2,1:T(1,128)S(1)}, u32[]{:S(2)}, u32[]{:S(2)}) %collective-permute-start.5) | collective-permute-done | bytes 7632 | tf_op jit(solution)/shard_map/ppermute | solution.py:57
  31.0 1.6 %copy.89 = f32[19,10,10,1]{3,2,1,0:T(8,128)S(1)} copy(f32[19,10,10,1]{0,3,2,1:T(1,128)S(1)} %collective-permute-done.5) | data formatting | bytes 15200 | tf_op jit(solution)/shard_map/ppermute | solution.py:57
  32.7 3.0 %collective-permute-done.4 = f32[19,10,10,1]{0,3,2,1:T(1,128)S(1)} collective-permute-done((f32[19,10,10,1]{0,3,2,1:T(1,128)S(1)}, f32[19,10,10,1]{0,3,2,1:T(1,128)S(1)}, u32[]{:S(2)}, u32[]{:S(2)}) %collective-permute-start.4) | collective-permute-done | bytes 7632 | tf_op jit(solution)/shard_map/ppermute | solution.py:55
  35.7 2.7 %copy.87 = f32[19,10,10,1]{3,2,1,0:T(8,128)} copy(f32[19,10,10,1]{0,3,2,1:T(1,128)S(1)} %collective-permute-done.4) | data formatting | bytes 15200 | tf_op jit(solution)/shard_map/ppermute | solution.py:55
  38.4 1.0 maximum_bitcast_fusion.13
  39.5 1.3 %copy-done.1 = f32[19,10,10,1]{3,2,1,0:T(8,128)S(1)} copy-done((f32[19,10,10,1]{3,2,1,0:T(8,128)S(1)}, f32[19,10,10,1]{3,2,1,0:T(8,128)}, u32[]{:S(2)}) %copy-start.1) | copy-done | bytes 7624
  48.6 2.1 %collective-permute-start.6 = (f32[19,1,8,128]{3,2,1,0:T(8,128)S(1)}, f32[19,1,8,128]{3,2,1,0:T(8,128)S(1)}, u32[]{:S(2)}, u32[]{:S(2)}) collective-permute-start(f32[19,1,8,128]{3,2,1,0:T(8,128)S(1)} %get-tuple-element.382), channel_id=1, source_target_pairs={{0,8},{8,16},{16,24},{24,0},{1,9},{9,17},{17,25},{25,1},{2,10},{10... | collective-permute-start | bytes 233480 | tf_op jit(solution)/shard_map/ppermute | solution.py:55
  51.6 2.4 %collective-permute-done.6 = f32[19,1,8,128]{3,2,1,0:T(8,128)S(1)} collective-permute-done((f32[19,1,8,128]{3,2,1,0:T(8,128)S(1)}, f32[19,1,8,128]{3,2,1,0:T(8,128)S(1)}, u32[]{:S(2)}, u32[]{:S(2)}) %collective-permute-start.6) | collective-permute-done | bytes 77856 | tf_op jit(solution)/shard_map/ppermute | solution.py:55
  53.9 1.2 %collective-permute-done.7 = f32[19,1,8,128]{3,2,1,0:T(8,128)S(1)} collective-permute-done((f32[19,1,8,128]{3,2,1,0:T(8,128)S(1)}, f32[19,1,8,128]{3,2,1,0:T(8,128)S(1)}, u32[]{:S(2)}, u32[]{:S(2)}) %collective-permute-start.7) | collective-permute-done | bytes 77856 | tf_op jit(solution)/shard_map/ppermute | solution.py:57
  57.1 1.7 %fusion.393 = (f32[19,10,10,1]{3,2,1,0:T(8,128)S(1)}, f32[19,10,10,1]{3,2,1,0:T(8,128)}) fusion(f32[19,10,10,128]{3,2,1,0:T(8,128)S(1)} %pad_maximum_fusion.1), kind=kLoop, calls=%fused_computation.695 | loop fusion | bytes 30400 | tf_op jit(solution)/shard_map/slice | solution.py:51
  58.8 2.1 %copy.90 = f32[19,10,10,1]{0,3,2,1:T(1,128)S(1)} copy(f32[19,10,10,1]{3,2,1,0:T(8,128)} %get-tuple-element.354) | data formatting | bytes 15200 | tf_op jit(solution)/shard_map/slice | solution.py:52
  61.0 1.4 %copy.92 = f32[19,10,10,1]{0,3,2,1:T(1,128)} copy(f32[19,10,10,1]{3,2,1,0:T(8,128)S(1)} %get-tuple-element.353) | data formatting | bytes 15200 | tf_op jit(solution)/shard_map/slice | solution.py:51
  62.4 3.8 %collective-permute-start.11 = (f32[19,10,10,1]{0,3,2,1:T(1,128)}, f32[19,10,10,1]{0,3,2,1:T(1,128)}, u32[]{:S(2)}, u32[]{:S(2)}) collective-permute-start(f32[19,10,10,1]{0,3,2,1:T(1,128)} %copy.92), channel_id=1, source_target_pairs={{1,0},{2,1},{3,2},{0,3},{5,4},{6,5},{7,6},{4,7},{9,8},{10,9},{11,1... | collective-permute-start | bytes 22808 | tf_op jit(solution)/shard_map/ppermute | solution.py:57
  66.9 1.6 %copy.91 = f32[19,10,10,1]{3,2,1,0:T(8,128)S(1)} copy(f32[19,10,10,1]{0,3,2,1:T(1,128)S(1)} %collective-permute-done.10) | data formatting | bytes 15200 | tf_op jit(solution)/shard_map/ppermute | solution.py:55
  68.6 3.4 %copy.93 = f32[19,10,10,1]{3,2,1,0:T(8,128)} copy(f32[19,10,10,1]{0,3,2,1:T(1,128)} %collective-permute-done.11) | data formatting | bytes 15200 | tf_op jit(solution)/shard_map/ppermute | solution.py:57
  72.1 1.0 maximum_bitcast_fusion.2
  73.1 0.9 constant_dynamic-update-slice_fusion.57
  77.7 1.4 %select_reduce_fusion = (f32[128]{0:T(128)}, f32[128]{0:T(128)}, f32[128]{0:T(128)}, f32[1,8,8,128]{3,2,1,0:T(8,128)S(1)}, f32[1,8,8,128]{3,2,1,0:T(8,128)S(1)},...) fusion(f32[8,8,128]{2,1,0:T(8,128)S(1)} %get-tuple-element.278,, ...), kind=kLoop, calls=%fused_computation.510 | loop fusion | flops 573056 | bytes 1612128 | tf_op jit(solution)/shard_map/reduce_sum | solution.py:133
  81.6 1.8 %all_gather.3 = f32[3,1,2,16]{3,1,0,2:T(1,128)S(1)} all-gather(f32[3,1,1,16]{3,1,0,2:T(1,128)S(1)} %fusion.364), channel_id=1, replica_groups=mesh['gz'=4,'gy'=2,'gx'=4] {'gy'}, dimensions={2}, use_global_device_ids=true | all-gather | bytes 576 | tf_op jit(solution)/shard_map/all_gather | solution.py:190
  83.5 3.8 %collective-permute-start.14 = (f32[3,1,2,16]{3,1,0,2:T(1,128)S(1)}, f32[3,1,2,16]{3,1,0,2:T(1,128)S(1)}, u32[]{:S(2)}, u32[]{:S(2)}) collective-permute-start(f32[3,1,2,16]{3,1,0,2:T(1,128)S(1)} %all_gather.3), channel_id=1, source_target_pairs={{1,0},{2,1},{3,2},{0,3},{5,4},{6,5},{7,6},{4,7},{9,8},{10,9},{11,1... | collective-permute-start | bytes 1160 | tf_op jit(solution)/shard_map/ppermute | solution.py:199
  92.2 5.3 %collective-permute-done.13 = f32[3,1,2,16]{3,1,0,2:T(1,128)S(1)} collective-permute-done((f32[3,1,2,16]{3,1,0,2:T(1,128)S(1)}, f32[3,1,2,16]{3,1,0,2:T(1,128)S(1)}, u32[]{:S(2)}, u32[]{:S(2)}) %collective-permute-start.13) | collective-permute-done | bytes 416 | tf_op jit(solution)/shard_map/ppermute | solution.py:197
  98.8 1.4 %multiply_subtract_fusion = f32[2,1,2,64]{3,2,1,0:T(2,128)} fusion(f32[2,1,2,64]{3,2,1,0:T(2,128)S(1)} %copy-done.8, f32[2,1,2,1]{3,2,1,0:T(2,128)} %get-tuple-element.399, f32[2,1,2,63]{3,2,1,0:T(2,128)} %get-tuple-element.401, f32[2,1,2,63]{3,2,1,0:T(2,128)} %get-tuple-element.400, f32[2,1,2,1]{3,2,1,0:T(2,128)} %get-tuple-element.398, ...), kind=kLoop, calls=%fused_computation.687 | loop fusion | flops 10496 | bytes 11810 | tf_op jit(solution)/shard_map/sub | solution.py:160
  (160 shorter events, 31.7 us)
Async XLA Ops:
  0.6 10.5 %copy-start.2 = (f32[19,8,8,128]{3,2,1,0:T(8,128)S(1)}, f32[19,8,8,128]{3,2,1,0:T(8,128)}, u32[]{:S(2)}) copy-start(f32[19,8,8,128]{3,2,1,0:T(8,128)} %param.53) | copy-start | bytes 1867780
  0.6 98.1 %collective-permute-start.15 = (f32[2,1,2,64]{3,2,1,0:T(2,128)}, f32[2,1,2,64]{3,2,1,0:T(2,128)}, u32[]{:S(2)}, u32[]{:S(2)}) collective-permute-start(f32[2,1,2,64]{3,2,1,0:T(2,128)} %param.56), channel_id=1, source_target_pairs={{0,8},{8,16},{16,24},{1,9},{9,17},{17,25},{2,10},{10,18},{18,26},{... | collective-permute-start | bytes 3080 | tf_op jit(solution)/shard_map/ppermute | solution.py:55
  6.2 92.6 %collective-permute-start.16 = (f32[2,1,2,64]{3,2,1,0:T(2,128)}, f32[2,1,2,64]{3,2,1,0:T(2,128)}, u32[]{:S(2)}, u32[]{:S(2)}) collective-permute-start(f32[2,1,2,64]{3,2,1,0:T(2,128)} %param.56), channel_id=1, source_target_pairs={{8,0},{16,8},{24,16},{9,1},{17,9},{25,17},{10,2},{18,10},{26,18},{... | collective-permute-start | bytes 3080 | tf_op jit(solution)/shard_map/ppermute | solution.py:57
  11.3 4.3 %copy-start.7 = (f32[2,1,2,64]{3,2,1,0:T(2,128)S(1)}, f32[2,1,2,64]{3,2,1,0:T(2,128)}, u32[]{:S(2)}) copy-start(f32[2,1,2,64]{3,2,1,0:T(2,128)} %param.56) | copy-start | bytes 3076
  11.3 4.9 %copy-start.14 = (f32[2,1,2,64]{3,2,1,0:T(2,128)S(1)}, f32[2,1,2,64]{3,2,1,0:T(2,128)}, u32[]{:S(2)}) copy-start(f32[2,1,2,64]{3,2,1,0:T(2,128)} %param.57) | copy-start | bytes 3076
  11.3 4.9 %copy-start.15 = (f32[2]{0:T(128)S(1)}, f32[2]{0:T(128)}, u32[]{:S(2)}) copy-start(f32[2]{0:T(128)} %constant.577.clone) | copy-start | bytes 28
  11.3 4.9 %copy-start.16 = (f32[2]{0:T(128)S(1)}, f32[2]{0:T(128)}, u32[]{:S(2)}) copy-start(f32[2]{0:T(128)} %constant.578.clone) | copy-start | bytes 28
  11.8 6.8 %collective-permute-start = (f32[19,1,8,128]{3,2,1,0:T(8,128)S(1)}, f32[19,1,8,128]{3,2,1,0:T(8,128)S(1)}, u32[]{:S(2)}, u32[]{:S(2)}) collective-permute-start(f32[19,1,8,128]{3,2,1,0:T(8,128)S(1)} %get-tuple-element.383), channel_id=1, source_target_pairs={{0,8},{8,16},{16,24},{24,0},{1,9},{9,17},{17,25},{25,1},{2,10},{10... | collective-permute-start | bytes 233480 | tf_op jit(solution)/shard_map/ppermute | solution.py:55
  14.5 5.0 %collective-permute-start.1 = (f32[19,1,8,128]{3,2,1,0:T(8,128)S(1)}, f32[19,1,8,128]{3,2,1,0:T(8,128)S(1)}, u32[]{:S(2)}, u32[]{:S(2)}) collective-permute-start(f32[19,1,8,128]{3,2,1,0:T(8,128)S(1)} %get-tuple-element.384), channel_id=1, source_target_pairs={{8,0},{16,8},{24,16},{0,24},{9,1},{17,9},{25,17},{1,25},{10,2},{18... | collective-permute-start | bytes 233480 | tf_op jit(solution)/shard_map/ppermute | solution.py:57
  19.7 1.4 %collective-permute-start.2 = (f32[19,10,1,128]{3,2,1,0:T(1,128)S(1)}, f32[19,10,1,128]{3,2,1,0:T(1,128)S(1)}, u32[]{:S(2)}, u32[]{:S(2)}) collective-permute-start(f32[19,10,1,128]{3,2,1,0:T(1,128)S(1)} %get-tuple-element.375), channel_id=1, source_target_pairs={{0,4},{4,0},{1,5},{5,1},{2,6},{6,2},{3,7},{7,3},{8,12},{12,8},{9,1... | collective-permute-start | bytes 291848 | tf_op jit(solution)/shard_map/ppermute | solution.py:55
  19.8 1.4 %collective-permute-start.3 = (f32[19,10,1,128]{3,2,1,0:T(1,128)S(1)}, f32[19,10,1,128]{3,2,1,0:T(1,128)S(1)}, u32[]{:S(2)}, u32[]{:S(2)}) collective-permute-start(f32[19,10,1,128]{3,2,1,0:T(1,128)S(1)} %get-tuple-element.376), channel_id=1, source_target_pairs={{4,0},{0,4},{5,1},{1,5},{6,2},{2,6},{7,3},{3,7},{12,8},{8,12},{13,... | collective-permute-start | bytes 291848 | tf_op jit(solution)/shard_map/ppermute | solution.py:57
  25.4 4.5 %copy-start.13 = (s32[2,8,128]{2,1,0:T(8,128)S(1)}, s32[2,8,128]{2,1,0:T(8,128)}, u32[]{:S(2)}) copy-start(s32[2,8,128]{2,1,0:T(8,128)} %param.55) | copy-start | bytes 24580
  25.4 5.6 %collective-permute-start.5 = (f32[19,10,10,1]{0,3,2,1:T(1,128)S(1)}, f32[19,10,10,1]{0,3,2,1:T(1,128)S(1)}, u32[]{:S(2)}, u32[]{:S(2)}) collective-permute-start(f32[19,10,10,1]{0,3,2,1:T(1,128)S(1)} %copy.88), channel_id=1, source_target_pairs={{1,0},{2,1},{3,2},{0,3},{5,4},{6,5},{7,6},{4,7},{9,8},{10,9},{11,1... | collective-permute-start | bytes 22808 | tf_op jit(solution)/shard_map/ppermute | solution.py:57
  29.8 5.9 %collective-permute-start.4 = (f32[19,10,10,1]{0,3,2,1:T(1,128)S(1)}, f32[19,10,10,1]{0,3,2,1:T(1,128)S(1)}, u32[]{:S(2)}, u32[]{:S(2)}) collective-permute-start(f32[19,10,10,1]{0,3,2,1:T(1,128)S(1)} %copy.86), channel_id=1, source_target_pairs={{0,1},{1,2},{2,3},{3,0},{4,5},{5,6},{6,7},{7,4},{8,9},{9,10},{10,1... | collective-permute-start | bytes 22808 | tf_op jit(solution)/shard_map/ppermute | solution.py:55
  29.9 11.0 %copy-start.9 = (pred[1,8,128]{2,1,0:T(8,128)(4,1)}, pred[1,8,128]{2,1,0:T(8,128)(4,1)S(1)}, u32[]{:S(2)}) copy-start(pred[1,8,128]{2,1,0:T(8,128)(4,1)S(1)} %get-tuple-element.317) | copy-start | bytes 3076
  39.4 1.4 %copy-start.1 = (f32[19,10,10,1]{3,2,1,0:T(8,128)S(1)}, f32[19,10,10,1]{3,2,1,0:T(8,128)}, u32[]{:S(2)}) copy-start(f32[19,10,10,1]{3,2,1,0:T(8,128)} %copy.87) | copy-start | bytes 22804
  48.6 5.3 %collective-permute-start.6 = (f32[19,1,8,128]{3,2,1,0:T(8,128)S(1)}, f32[19,1,8,128]{3,2,1,0:T(8,128)S(1)}, u32[]{:S(2)}, u32[]{:S(2)}) collective-permute-start(f32[19,1,8,128]{3,2,1,0:T(8,128)S(1)} %get-tuple-element.382), channel_id=1, source_target_pairs={{0,8},{8,16},{16,24},{24,0},{1,9},{9,17},{17,25},{25,1},{2,10},{10... | collective-permute-start | bytes 233480 | tf_op jit(solution)/shard_map/ppermute | solution.py:55
  50.7 4.4 %collective-permute-start.7 = (f32[19,1,8,128]{3,2,1,0:T(8,128)S(1)}, f32[19,1,8,128]{3,2,1,0:T(8,128)S(1)}, u32[]{:S(2)}, u32[]{:S(2)}) collective-permute-start(f32[19,1,8,128]{3,2,1,0:T(8,128)S(1)} %get-tuple-element.381), channel_id=1, source_target_pairs={{8,0},{16,8},{24,16},{0,24},{9,1},{17,9},{25,17},{1,25},{10,2},{18... | collective-permute-start | bytes 233480 | tf_op jit(solution)/shard_map/ppermute | solution.py:57
  55.2 1.4 %collective-permute-start.8 = (f32[19,10,1,128]{3,2,1,0:T(1,128)S(1)}, f32[19,10,1,128]{3,2,1,0:T(1,128)S(1)}, u32[]{:S(2)}, u32[]{:S(2)}) collective-permute-start(f32[19,10,1,128]{3,2,1,0:T(1,128)S(1)} %get-tuple-element.371), channel_id=1, source_target_pairs={{0,4},{4,0},{1,5},{5,1},{2,6},{6,2},{3,7},{7,3},{8,12},{12,8},{9,1... | collective-permute-start | bytes 291848 | tf_op jit(solution)/shard_map/ppermute | solution.py:55
  55.3 1.4 %collective-permute-start.9 = (f32[19,10,1,128]{3,2,1,0:T(1,128)S(1)}, f32[19,10,1,128]{3,2,1,0:T(1,128)S(1)}, u32[]{:S(2)}, u32[]{:S(2)}) collective-permute-start(f32[19,10,1,128]{3,2,1,0:T(1,128)S(1)} %get-tuple-element.372), channel_id=1, source_target_pairs={{4,0},{0,4},{5,1},{1,5},{6,2},{2,6},{7,3},{3,7},{12,8},{8,12},{13,... | collective-permute-start | bytes 291848 | tf_op jit(solution)/shard_map/ppermute | solution.py:57
  60.9 6.0 %collective-permute-start.10 = (f32[19,10,10,1]{0,3,2,1:T(1,128)S(1)}, f32[19,10,10,1]{0,3,2,1:T(1,128)S(1)}, u32[]{:S(2)}, u32[]{:S(2)}) collective-permute-start(f32[19,10,10,1]{0,3,2,1:T(1,128)S(1)} %copy.90), channel_id=1, source_target_pairs={{0,1},{1,2},{2,3},{3,0},{4,5},{5,6},{6,7},{7,4},{8,9},{9,10},{10,1... | collective-permute-start | bytes 22808 | tf_op jit(solution)/shard_map/ppermute | solution.py:55
  62.4 6.3 %collective-permute-start.11 = (f32[19,10,10,1]{0,3,2,1:T(1,128)}, f32[19,10,10,1]{0,3,2,1:T(1,128)}, u32[]{:S(2)}, u32[]{:S(2)}) collective-permute-start(f32[19,10,10,1]{0,3,2,1:T(1,128)} %copy.92), channel_id=1, source_target_pairs={{1,0},{2,1},{3,2},{0,3},{5,4},{6,5},{7,6},{4,7},{9,8},{10,9},{11,1... | collective-permute-start | bytes 22808 | tf_op jit(solution)/shard_map/ppermute | solution.py:57
  72.1 1.0 %copy-start.10 = (pred[1,8,128]{2,1,0:T(8,128)(4,1)S(1)}, pred[1,8,128]{2,1,0:T(8,128)(4,1)}, u32[]{:S(2)}) copy-start(pred[1,8,128]{2,1,0:T(8,128)(4,1)} %copy-done.9) | copy-start | bytes 3076
  73.1 1.6 %copy-start = (f32[19,10,10,1]{3,2,1,0:T(8,128)S(1)}, f32[19,10,10,1]{3,2,1,0:T(8,128)}, u32[]{:S(2)}) copy-start(f32[19,10,10,1]{3,2,1,0:T(8,128)} %copy.93) | copy-start | bytes 22804
  74.0 1.5 %copy-start.12 = (pred[1,8,128]{2,1,0:T(8,128)(4,1)S(1)}, pred[1,8,128]{2,1,0:T(8,128)(4,1)}, u32[]{:S(2)}) copy-start(pred[1,8,128]{2,1,0:T(8,128)(4,1)} %copy-done.11) | copy-start | bytes 3076
  74.7 3.0 %copy-start.5 = (f32[8,8,128]{2,1,0:T(8,128)}, f32[8,8,128]{2,1,0:T(8,128)S(1)}, u32[]{:S(2)}) copy-start(f32[8,8,128]{2,1,0:T(8,128)S(1)} %constant_dynamic-update-slice_fusion.61) | copy-start | bytes 98308
  76.2 1.4 %copy-start.6 = (s32[8,8,128]{2,1,0:T(8,128)S(1)}, s32[8,8,128]{2,1,0:T(8,128)}, u32[]{:S(2)}) copy-start(s32[8,8,128]{2,1,0:T(8,128)} %param.54) | copy-start | bytes 98308
  77.7 21.1 %copy-start.8 = (f32[2,1,2,64]{3,2,1,0:T(2,128)S(1)}, f32[2,1,2,64]{3,2,1,0:T(2,128)}, u32[]{:S(2)}) copy-start(f32[2,1,2,64]{3,2,1,0:T(2,128)} %param.56) | copy-start | bytes 3076
  83.5 8.5 %collective-permute-start.12 = (f32[3,1,2,16]{3,1,0,2:T(1,128)S(1)}, f32[3,1,2,16]{3,1,0,2:T(1,128)S(1)}, u32[]{:S(2)}, u32[]{:S(2)}) collective-permute-start(f32[3,1,2,16]{3,1,0,2:T(1,128)S(1)} %all_gather.3), channel_id=1, source_target_pairs={{0,1},{1,2},{2,3},{3,0},{4,5},{5,6},{6,7},{7,4},{8,9},{9,10},{10,1... | collective-permute-start | bytes 1160 | tf_op jit(solution)/shard_map/ppermute | solution.py:197
  83.5 8.6 %collective-permute-start.14 = (f32[3,1,2,16]{3,1,0,2:T(1,128)S(1)}, f32[3,1,2,16]{3,1,0,2:T(1,128)S(1)}, u32[]{:S(2)}, u32[]{:S(2)}) collective-permute-start(f32[3,1,2,16]{3,1,0,2:T(1,128)S(1)} %all_gather.3), channel_id=1, source_target_pairs={{1,0},{2,1},{3,2},{0,3},{5,4},{6,5},{7,6},{4,7},{9,8},{10,9},{11,1... | collective-permute-start | bytes 1160 | tf_op jit(solution)/shard_map/ppermute | solution.py:199
  92.0 5.4 %collective-permute-start.13 = (f32[3,1,2,16]{3,1,0,2:T(1,128)S(1)}, f32[3,1,2,16]{3,1,0,2:T(1,128)S(1)}, u32[]{:S(2)}, u32[]{:S(2)}) collective-permute-start(f32[3,1,2,16]{3,1,0,2:T(1,128)S(1)} %collective-permute-done.12), channel_id=1, source_target_pairs={{0,1},{1,2},{2,3},{3,0},{4,5},{5,6},{6,7},{7,4},{8,9},{9,10},{10,1... | collective-permute-start | bytes 1160 | tf_op jit(solution)/shard_map/ppermute | solution.py:197
  92.1 8.2 %copy-start.3 = (f32[19,8,8,128]{3,2,1,0:T(8,128)}, f32[19,8,8,128]{3,2,1,0:T(8,128)S(1)}, u32[]{:S(2)}) copy-start(f32[19,8,8,128]{3,2,1,0:T(8,128)S(1)} %constant_dynamic-update-slice_fusion.38) | copy-start | bytes 1867780
  (2 other events, 1.5 us)
